TPU v7x, 512 devices: a whole 4x4x16 slice. The times are simulated.
512 devices in a mesh: pair: 16 (over y, z_lo), task: 32 (over z_hi, x, core).
Axes of the slice: x: 4, y: 4, z: 16 (z_hi: 4, z_lo: 4; z = z_hi * 4 + z_lo), core: 2. Of those that a mesh axis runs over, the one named last changes fastest.
Arguments:
- factor_blocks: bfloat16 [64, 1536, 625], P('task', 'pair'), may hold values from -1.25 to 1.25
- amplitudes: bfloat16 [64, 512, 625], P('task', 'pair'), may hold values from -0.15625 to 0.15625
- residual_in: float32 [64, 512, 625], P('task', 'pair'), may hold values from -6 to 6
- task_owners: int32 [512, 3], replicated, may hold values from 0 to 31, all different within a row; in each aligned block of 16 rows (0 to 15, 16 to 31, ...) at most 2 rows name the same one
- task_local: int32 [512, 4], replicated, may hold values from 0 to 1
Outputs:
- residual_out: float32 [64, 512, 625], P('task', 'pair')
Inputs may be any that keep to these rules, and one draw needn't show every extreme that they name: `task_owners`: the three numbers of a row differ; in each aligned block of 16 rows no number appears more than 2 times.
All inputs are finite; a program needn't handle non-finite values.
Results may differ from a plain program's by a relative error of at most 0.012.
Values may be sent and summed in bfloat16 or wider, within the bound.
A program may use at most 64 MiB of HBM per device.

v0:
```python
import jax
import jax.numpy as jnp
from jax import lax
from jax.sharding import PartitionSpec as P

TV = 25


def per_device(factor_blocks, amplitudes, residual_in, task_owners, task_local):
    pair_count = lax.axis_size("pair")
    task_count = lax.axis_size("task")
    helper = lax.axis_index("pair")
    column = lax.axis_index("task")
    blocks_here = factor_blocks.shape[0]
    tile_width = factor_blocks.shape[2]
    owners_all = task_owners.reshape(task_count, pair_count, 3)
    local_all = task_local.reshape(task_count, pair_count, 4)
    my_owners = lax.dynamic_index_in_dim(owners_all, column, 0, keepdims=False)
    my_local = lax.dynamic_index_in_dim(local_all, column, 0, keepdims=False)
    zero_value = jnp.zeros((), factor_blocks.dtype)
    factor_all, amps_all = (
        lax.all_gather(factor_blocks, "task", axis=0, tiled=True),
        lax.all_gather(amplitudes, "task", axis=0, tiled=True),
    )
    global_ids = my_owners * blocks_here + my_local[:, :3]
    factor_send = jnp.stack([factor_all[global_ids[:, 0]], factor_all[global_ids[:, 1]]], axis=0)
    amp_send = amps_all[global_ids[:, 2]][None]
    factor_recv, amp_recv = (
        lax.all_to_all(factor_send, "pair", split_axis=1, concat_axis=1, tiled=True),
        lax.all_to_all(amp_send, "pair", split_axis=1, concat_axis=1, tiled=True),
    )
    row_factor = factor_recv[0].reshape(-1, tile_width)
    col_factor = factor_recv[1].reshape(-1, tile_width)
    amp_block = amp_recv[0].reshape(-1, tile_width)
    integral_tile = lax.dot_general(
        row_factor, col_factor, (((0,), (0,)), ((), ())), preferred_element_type=jnp.float32
    ).astype(jnp.bfloat16)
    ladder = jnp.einsum(
        "icd,acbd->iab",
        amp_block.reshape(-1, TV, TV),
        integral_tile.reshape(TV, TV, TV, TV),
        preferred_element_type=jnp.float32,
    )
    ladder = ladder.astype(jnp.bfloat16).reshape(-1, tile_width)
    onehot = my_local[:, 3][None, :] == jnp.arange(blocks_here, dtype=jnp.int32)[:, None]
    my_target = lax.dynamic_index_in_dim(onehot, helper, 1, keepdims=False)
    partials = jnp.where(my_target[:, None, None], ladder[None], zero_value)
    block_sums = lax.psum_scatter(partials, "pair", scatter_dimension=1, tiled=True).astype(
        jnp.float32
    )
    return residual_in + block_sums


def solution(mesh):
    placed = (P("task", "pair", None), P("task", "pair", None), P("task", "pair", None), P(), P())
    return jax.shard_map(
        per_device, mesh=mesh, in_specs=placed, out_specs=P("task", "pair", None), check_vma=False
    )
```

profile of v0, /device:TPU:2, one launch (start us, length us, event | category | flops | bytes accessed | tf_op | source)
XLA Modules:
  0.0 456.9 jit_solution(9482900807218954983)
XLA Ops:
  6.5 0.0 all-gather.3.cloned.1.call-start
  6.5 0.7 all-gather.3.cloned.1.call-update
  7.3 0.0 all-gather.5.cloned.1.call-start
  7.3 0.7 all-gather.5.cloned.1.call-update
  8.0 0.8 reshape.21
  8.8 0.8 reshape.22
  9.7 87.8 %all-gather.3.cloned.1.call-done = bf16[64,32,625]{2,1,0:T(8,128)(2,1)} async-done(((bf16[2,32,625]{2,1,0:T(8,128)(2,1)}), bf16[64,32,625]{2,1,0:T(8,128)(2,1)}) %all-gather.3.cloned.1.call-update) | async-done | bytes 2560016 | tf_op jit(solution)/shard_map/all_gather | solution.py:23
  97.5 3.2 gather_fusion
  100.7 4.9 %all-to-all-start = ((bf16[1,16,32,625]{3,2,0,1:T(8,128)(2,1)}), bf16[1,16,32,625]{3,2,0,1:T(8,128)(2,1)S(1)}, u32[]{:S(2)}, u32[]{:S(2)}) async-start(bf16[1,16,32,625]{3,2,0,1:T(8,128)(2,1)} %bitcast.5), calls=%async_computation | async-start | bytes 1310720 | tf_op jit(solution)/shard_map/all_to_all | solution.py:30
  105.6 122.4 %all-gather.5.cloned.1.call-done = bf16[64,96,625]{2,1,0:T(8,128)(2,1)} async-done(((bf16[2,96,625]{2,1,0:T(8,128)(2,1)}), bf16[64,96,625]{2,1,0:T(8,128)(2,1)}) %all-gather.5.cloned.1.call-update) | async-done | bytes 7680016 | tf_op jit(solution)/shard_map/all_gather | solution.py:22
  228.0 4.1 gather_fusion.1
  232.1 5.4 %gather_fusion.2 = bf16[16,96,625]{2,1,0:T(8,128)(2,1)} fusion(bf16[64,96,625]{2,1,0:T(8,128)(2,1)} %all-gather.5.cloned.1.call-done, s32[1024]{0:T(1024)S(1)} %get-tuple-element.8), kind=kCustom, calls=%fused_computation.2 | custom fusion | bytes 3840064 | tf_op jit(solution)/shard_map/gather | solution.py:26
  237.5 2.1 pad_maximum_fusion
  239.6 2.5 copy.14
  242.1 0.0 all-to-all-done
  242.1 4.5 all-to-all-start.1
  246.7 0.2 reduce-scatter.2.cloned.1.call-start
  246.9 0.6 dynamic-slice
  247.5 0.7 compare_bitcast_fusion
  248.2 3.5 copy.13
  251.7 3.5 reshape.51
  255.2 83.2 %all-to-all-done.1 = bf16[2,16,96,625]{3,2,0,1:T(8,128)(2,1)} async-done(((bf16[2,16,96,625]{3,2,0,1:T(8,128)(2,1)}), bf16[2,16,96,625]{3,2,0,1:T(8,128)(2,1)}, u32[]{:S(2)}, u32[]{:S(2)}) %all-to-all-start.1) | async-done | bytes 3840032 | tf_op jit(solution)/shard_map/all_to_all | solution.py:29
  338.3 3.9 bitcast_convert_fusion.1
  342.2 0.0 copy-start
  342.2 12.5 %reshape.25 = bf16[25,25,25,25]{3,2,1,0:T(8,128)(2,1)} reshape(bf16[625,625]{1,0:T(8,128)(2,1)S(1)} %bitcast_convert_fusion.1) | data formatting | bytes 1562500 | tf_op jit(solution)/shard_map/reshape | solution.py:41
  354.7 0.0 copy-done
  354.7 3.6 bitcast_convert_fusion
  358.3 0.2 broadcast_in_dim.35
  358.5 0.3 copy.17
  358.8 0.0 copy-start.1
  358.8 1.3 broadcast_select_fusion
  360.1 0.0 reduce-scatter.2.cloned.1.call-update
  360.1 88.7 %reduce-scatter.2.cloned.1.call-done = bf16[2,32,625]{2,1,0:T(8,128)(2,1)} async-done(((bf16[2,512,625]{2,1,0:T(8,128)(2,1)}), bf16[2,32,625]{2,1,0:T(8,128)(2,1)}) %reduce-scatter.2.cloned.1.call-update) | async-done | bytes 80016 | tf_op jit(solution)/shard_map/reduce_scatter | solution.py:48
  448.7 0.0 copy-done.1
  448.8 1.6 convert_add_fusion
  (7 shorter events, 0.1 us)
Async XLA Ops:
  6.5 90.9 %all-gather.3.cloned.1.call-start = ((), (), s32[]{:S(2)}) async-start(), calls=%async_computation.3 | async-start | bytes 2703360 | tf_op jit(solution)/shard_map/all_gather | solution.py:23
  7.3 220.7 %all-gather.5.cloned.1.call-start = ((), (), s32[]{:S(2)}) async-start(), calls=%async_computation.4 | async-start | bytes 8110080 | tf_op jit(solution)/shard_map/all_gather | solution.py:22
  100.7 141.5 %all-to-all-start = ((bf16[1,16,32,625]{3,2,0,1:T(8,128)(2,1)}), bf16[1,16,32,625]{3,2,0,1:T(8,128)(2,1)S(1)}, u32[]{:S(2)}, u32[]{:S(2)}) async-start(bf16[1,16,32,625]{3,2,0,1:T(8,128)(2,1)} %bitcast.5), calls=%async_computation | async-start | bytes 1310720 | tf_op jit(solution)/shard_map/all_to_all | solution.py:30
  242.1 96.2 %all-to-all-start.1 = ((bf16[2,16,96,625]{3,2,0,1:T(8,128)(2,1)}), bf16[2,16,96,625]{3,2,0,1:T(8,128)(2,1)}, u32[]{:S(2)}, u32[]{:S(2)}) async-start(bf16[2,16,96,625]{3,2,0,1:T(8,128)(2,1)} %copy.14), calls=%async_computation.1 | async-start | bytes 7864320 | tf_op jit(solution)/shard_map/all_to_all | solution.py:29
  246.7 202.1 %reduce-scatter.2.cloned.1.call-start = ((), (), s32[]{:S(2)}) async-start(), calls=%async_computation.5 | async-start | bytes 1392640 | tf_op jit(solution)/shard_map/reduce_scatter | solution.py:48
  342.2 12.5 %copy-start = (bf16[512,25,25,1]{0,2,1,3:T(8,128)(2,1)S(1)}, bf16[512,25,25,1]{0,2,1,3:T(8,128)(2,1)}, u32[]{:S(2)}) copy-start(bf16[512,25,25,1]{0,2,1,3:T(8,128)(2,1)} %reshape.51) | copy-start | bytes 1920004
  358.8 90.0 %copy-start.1 = (f32[2,32,625]{2,1,0:T(8,128)S(1)}, f32[2,32,625]{2,1,0:T(8,128)}, u32[]{:S(2)}) copy-start(f32[2,32,625]{2,1,0:T(8,128)} %param.7) | copy-start | bytes 480004
Sparse Core Ops, SparseCore 0:
  10.5 86.9 all-gather.2
  100.6 127.3 all-gather.4
  360.2 88.5 reduce-scatter.1
where the time goes:
time: 457 us
  waiting for transfers between devices  383 us (84%)
  local copies, waits for them, and re-layouts  37.3 us (8%)
  between operations  13.3 us (3%)
  starting transfers between devices  9.73 us (2%)
  matrix products  7.45 us (2%)
  other arithmetic  5.64 us (1%)
    all_gather x1, waiting for transfers between devices, per_device(): lax.all_gather(factor_blocks, 'task', axis=0, tiled=True)  122 us
    reduce_scatter x1, waiting for transfers between devices, per_device(): lax.psum_scatter(partials, 'pair', scatter_dimension=1, tiled=True)  88.7 us
    all_gather x1, waiting for transfers between devices, per_device(): lax.all_gather(amplitudes, 'task', axis=0, tiled=True)  87.8 us
    all_to_all x1, waiting for transfers between devices, per_device(): lax.all_to_all(factor_send, 'pair', split_axis=1, concat_axis=1, tiled=True)  83.2 us
    reshape x1, local copies, waits for them, and re-layouts, per_device(): integral_tile.reshape(TV, TV, TV, TV)  12.5 us
  transfers between devices with their start and end apart: 5, of which 4 were waited for; matrix products, arithmetic and copies ran while one was open for 6% of the time, Pallas kernels for 0%

commit v1 on v0

--- a/solution.py
+++ b/solution.py
@@ -20,7 +20,9 @@
     zero_value = jnp.zeros((), factor_blocks.dtype)
     factor_all, amps_all = (
         lax.all_gather(factor_blocks, "task", axis=0, tiled=True),
-        lax.all_gather(amplitudes, "task", axis=0, tiled=True),
+        jnp.concatenate(
+            lax.all_to_all(jnp.stack([amplitudes] * lax.axis_size("task")), "task", 0, 0), axis=0
+        ),
     )
     global_ids = my_owners * blocks_here + my_local[:, :3]
     factor_send = jnp.stack([factor_all[global_ids[:, 0]], factor_all[global_ids[:, 1]]], axis=0)

time: 457 us -> 476 us (1.042)
  the two profiles are of different devices: /device:TPU:2 before, /device:TPU:6 now
where the time goes in v1:
time: 476 us; the launch traced here: 475 us
  waiting for transfers between devices  358 us (75%)
  starting transfers between devices  53 us (11%)
  local copies, waits for them, and re-layouts  37 us (8%)
  between operations  13.6 us (3%)
  matrix products  7.46 us (2%)
  other arithmetic  5.64 us (1%)
    all_to_all x1, waiting for transfers between devices, per_device(): lax.all_to_all(jnp.stack([amplitudes] * lax.axis_size('task')), 'task', 0...  144 us
    reduce_scatter x1, waiting for transfers between devices, per_device(): lax.psum_scatter(partials, 'pair', scatter_dimension=1, tiled=True)  86.5 us
    all_to_all x1, waiting for transfers between devices, per_device(): lax.all_to_all(factor_send, 'pair', split_axis=1, concat_axis=1, tiled=True)  82.9 us
    all_gather x1, waiting for transfers between devices, per_device(): lax.all_gather(factor_blocks, 'task', axis=0, tiled=True)  44.1 us
    all_to_all x1, starting transfers between devices, per_device(): lax.all_to_all(factor_send, 'pair', split_axis=1, concat_axis=1, tiled=True)  25.7 us
    all_to_all x1, starting transfers between devices, per_device(): lax.all_to_all(jnp.stack([amplitudes] * lax.axis_size('task')), 'task', 0...  18.3 us
    reshape x1, local copies, waits for them, and re-layouts, per_device(): integral_tile.reshape(TV, TV, TV, TV)  12.5 us
  transfers between devices with their start and end apart: 5, of which 4 were waited for; matrix products, arithmetic and copies ran while one was open for 6% of the time, Pallas kernels for 0%

profile of v1, /device:TPU:6, one launch (start us, length us, event | category | flops | bytes accessed | tf_op | source)
XLA Modules:
  0.0 475.1 jit_solution(1518794759411097529)
XLA Ops:
  6.5 0.0 all-gather.2.cloned.1.call-start
  6.5 0.7 all-gather.2.cloned.1.call-update
  7.3 2.8 stack.8
  10.1 0.0 copy-start.2
  10.1 0.0 copy-start.3
  10.1 18.3 %all-to-all-start = ((bf16[32,2,32,625]{3,2,1,0:T(8,128)(2,1)}), bf16[32,2,32,625]{3,2,1,0:T(8,128)(2,1)S(1)}, u32[]{:S(2)}, u32[]{:S(2)}) async-start(bf16[32,2,32,625]{3,2,1,0:T(8,128)(2,1)} %stack.8), calls=%async_computation | async-start | bytes 5242880 | tf_op jit(solution)/shard_map/all_to_all | solution.py:24
  28.4 0.0 copy-done.2
  28.4 0.1 reshape.26
  28.5 0.0 copy-done.3
  28.5 0.1 reshape.28
  28.7 144.1 %all-to-all-done = bf16[32,2,32,625]{3,2,1,0:T(8,128)(2,1)S(1)} async-done(((bf16[32,2,32,625]{3,2,1,0:T(8,128)(2,1)}), bf16[32,2,32,625]{3,2,1,0:T(8,128)(2,1)S(1)}, u32[]{:S(2)}, u32[]{:S(2)}) %all-to-all-start) | async-done | bytes 2560032 | tf_op jit(solution)/shard_map/all_to_all | solution.py:24
  172.8 1.5 gather_fusion
  174.3 8.8 %all-to-all-start.1 = ((bf16[1,16,32,625]{3,2,0,1:T(8,128)(2,1)}), bf16[1,16,32,625]{3,2,0,1:T(8,128)(2,1)S(1)}, u32[]{:S(2)}, u32[]{:S(2)}) async-start(bf16[1,16,32,625]{3,2,0,1:T(8,128)(2,1)} %bitcast.6), calls=%async_computation.1 | async-start | bytes 1310720 | tf_op jit(solution)/shard_map/all_to_all | solution.py:32
  183.1 44.1 %all-gather.2.cloned.1.call-done = bf16[64,96,625]{2,1,0:T(8,128)(2,1)} async-done(((bf16[2,96,625]{2,1,0:T(8,128)(2,1)}), bf16[64,96,625]{2,1,0:T(8,128)(2,1)}) %all-gather.2.cloned.1.call-update) | async-done | bytes 7680016 | tf_op jit(solution)/shard_map/all_gather | solution.py:22
  227.2 4.1 gather_fusion.2
  231.3 5.4 %gather_fusion.1 = bf16[16,96,625]{2,1,0:T(8,128)(2,1)} fusion(bf16[64,96,625]{2,1,0:T(8,128)(2,1)} %all-gather.2.cloned.1.call-done, s32[1024]{0:T(1024)S(1)} %get-tuple-element.9), kind=kCustom, calls=%fused_computation.1 | custom fusion | bytes 3840064 | tf_op jit(solution)/shard_map/gather | solution.py:28
  236.7 2.1 pad_maximum_fusion
  238.8 2.5 copy.13
  241.3 0.0 all-to-all-done.1
  241.3 25.7 %all-to-all-start.2 = ((bf16[2,16,96,625]{3,2,0,1:T(8,128)(2,1)}), bf16[2,16,96,625]{3,2,0,1:T(8,128)(2,1)}, u32[]{:S(2)}, u32[]{:S(2)}) async-start(bf16[2,16,96,625]{3,2,0,1:T(8,128)(2,1)} %copy.13), calls=%async_computation.2 | async-start | bytes 7864320 | tf_op jit(solution)/shard_map/all_to_all | solution.py:31
  267.0 0.2 reduce-scatter.2.cloned.1.call-start
  267.2 0.6 dynamic-slice
  267.8 0.7 compare_bitcast_fusion
  268.5 3.5 copy.12
  272.0 3.5 reshape.57
  275.5 82.9 %all-to-all-done.2 = bf16[2,16,96,625]{3,2,0,1:T(8,128)(2,1)} async-done(((bf16[2,16,96,625]{3,2,0,1:T(8,128)(2,1)}), bf16[2,16,96,625]{3,2,0,1:T(8,128)(2,1)}, u32[]{:S(2)}, u32[]{:S(2)}) %all-to-all-start.2) | async-done | bytes 3840032 | tf_op jit(solution)/shard_map/all_to_all | solution.py:31
  358.4 3.9 bitcast_convert_fusion.1
  362.2 0.0 copy-start
  362.2 12.5 %reshape.31 = bf16[25,25,25,25]{3,2,1,0:T(8,128)(2,1)} reshape(bf16[625,625]{1,0:T(8,128)(2,1)S(1)} %bitcast_convert_fusion.1) | data formatting | bytes 1562500 | tf_op jit(solution)/shard_map/reshape | solution.py:43
  374.7 0.0 copy-done
  374.7 3.6 bitcast_convert_fusion
  378.3 0.2 broadcast_in_dim.35
  378.5 0.0 copy-start.1
  378.5 0.3 copy.16
  378.8 1.3 broadcast_select_fusion
  380.1 0.0 reduce-scatter.2.cloned.1.call-update
  380.1 86.5 %reduce-scatter.2.cloned.1.call-done = bf16[2,32,625]{2,1,0:T(8,128)(2,1)} async-done(((bf16[2,512,625]{2,1,0:T(8,128)(2,1)}), bf16[2,32,625]{2,1,0:T(8,128)(2,1)}) %reduce-scatter.2.cloned.1.call-update) | async-done | bytes 80016 | tf_op jit(solution)/shard_map/reduce_scatter | solution.py:50
  466.7 0.0 copy-done.1
  466.7 1.6 convert_add_fusion
  (7 shorter events, 0.1 us)
Async XLA Ops:
  6.5 220.6 %all-gather.2.cloned.1.call-start = ((), (), s32[]{:S(2)}) async-start(), calls=%async_computation.4 | async-start | bytes 8110080 | tf_op jit(solution)/shard_map/all_gather | solution.py:22
  10.1 18.3 %copy-start.2 = (s32[512,4]{0,1:T(4,128)S(1)}, s32[512,4]{0,1:T(4,128)}, u32[]{:S(2)}) copy-start(s32[512,4]{0,1:T(4,128)} %param.9) | copy-start | bytes 24580
  10.1 18.4 %copy-start.3 = (s32[512,3]{0,1:T(4,128)S(1)}, s32[512,3]{0,1:T(4,128)}, u32[]{:S(2)}) copy-start(s32[512,3]{0,1:T(4,128)} %param.8) | copy-start | bytes 18436
  10.1 162.7 %all-to-all-start = ((bf16[32,2,32,625]{3,2,1,0:T(8,128)(2,1)}), bf16[32,2,32,625]{3,2,1,0:T(8,128)(2,1)S(1)}, u32[]{:S(2)}, u32[]{:S(2)}) async-start(bf16[32,2,32,625]{3,2,1,0:T(8,128)(2,1)} %stack.8), calls=%async_computation | async-start | bytes 5242880 | tf_op jit(solution)/shard_map/all_to_all | solution.py:24
  174.3 67.0 %all-to-all-start.1 = ((bf16[1,16,32,625]{3,2,0,1:T(8,128)(2,1)}), bf16[1,16,32,625]{3,2,0,1:T(8,128)(2,1)S(1)}, u32[]{:S(2)}, u32[]{:S(2)}) async-start(bf16[1,16,32,625]{3,2,0,1:T(8,128)(2,1)} %bitcast.6), calls=%async_computation.1 | async-start | bytes 1310720 | tf_op jit(solution)/shard_map/all_to_all | solution.py:32
  241.3 117.1 %all-to-all-start.2 = ((bf16[2,16,96,625]{3,2,0,1:T(8,128)(2,1)}), bf16[2,16,96,625]{3,2,0,1:T(8,128)(2,1)}, u32[]{:S(2)}, u32[]{:S(2)}) async-start(bf16[2,16,96,625]{3,2,0,1:T(8,128)(2,1)} %copy.13), calls=%async_computation.2 | async-start | bytes 7864320 | tf_op jit(solution)/shard_map/all_to_all | solution.py:31
  267.0 199.7 %reduce-scatter.2.cloned.1.call-start = ((), (), s32[]{:S(2)}) async-start(), calls=%async_computation.5 | async-start | bytes 1392640 | tf_op jit(solution)/shard_map/reduce_scatter | solution.py:50
  362.2 12.5 %copy-start = (bf16[512,25,25,1]{0,2,1,3:T(8,128)(2,1)S(1)}, bf16[512,25,25,1]{0,2,1,3:T(8,128)(2,1)}, u32[]{:S(2)}) copy-start(bf16[512,25,25,1]{0,2,1,3:T(8,128)(2,1)} %reshape.57) | copy-start | bytes 1920004
  378.5 88.1 %copy-start.1 = (f32[2,32,625]{2,1,0:T(8,128)S(1)}, f32[2,32,625]{2,1,0:T(8,128)}, u32[]{:S(2)}) copy-start(f32[2,32,625]{2,1,0:T(8,128)} %param.7) | copy-start | bytes 480004
Sparse Core Ops, SparseCore 0:
  10.5 216.6 all-gather.1
  380.2 86.3 reduce-scatter.1
